TPU v7x, 32 devices: a whole 2x2x4 slice. The times are simulated.
32 devices in a mesh: fsdp: 2 (over core), ctx: 4 (over y, x), tp: 4 (over z).
Axes of the slice: x: 2, y: 2, z: 4, core: 2. Of those that a mesh axis runs over, the one named last changes fastest.
Arguments:
- layer_input: float32 [4, 1024, 512], P('fsdp', 'ctx'), may hold values from -6 to 6
- timesteps: int32 [4], P('fsdp'), may hold values from 0 to 999
- segment_ids: int32 [4, 1024], P('fsdp'), may hold values from 0 to 15, never falling along the last dimension, each value on 1 to 512 neighbouring positions
- time_table: float32 [1000, 512], replicated, may hold values from -3 to 3
- ln1_gain: float32 [512], replicated, may hold values from 0.5 to 1.5
- ln1_bias: float32 [512], replicated, may hold values from -1.5 to 1.5
- w_qkv: float32 [3, 512, 512], P(None, 'fsdp', 'tp'), may hold values from -0.25 to 0.25
- b_qv: float32 [2, 512], P(None, 'tp'), may hold values from -1.5 to 1.5
- w_out_t: float32 [512, 512], P('fsdp', 'tp'), may hold values from -1 to 1
- b_out: float32 [512], replicated, may hold values from -1.5 to 1.5
- ln2_gain: float32 [512], replicated, may hold values from 0.5 to 1.5
- ln2_bias: float32 [512], replicated, may hold values from -1.5 to 1.5
- w_up: float32 [512, 2048], P('fsdp', 'tp'), may hold values from -0.25 to 0.25
- b_up: float32 [2048], P('tp'), may hold values from -1.5 to 1.5
- w_down_t: float32 [512, 2048], P('fsdp', 'tp'), may hold values from -0.125 to 0.125
- b_down: float32 [512], replicated, may hold values from -1.5 to 1.5
- out_grad: float32 [4, 1024, 512], P('fsdp', 'ctx'), may hold values from -6 to 6
Outputs:
- output: float32 [4, 1024, 512], P('fsdp', 'ctx')
- grad_input: float32 [4, 1024, 512], P('fsdp', 'ctx')
- grad_table: float32 [1000, 512], replicated
- grad_ln1_gain: float32 [512], replicated
- grad_ln1_bias: float32 [512], replicated
- grad_w_qkv: float32 [3, 512, 512], P(None, 'fsdp', 'tp')
- grad_b_qv: float32 [2, 512], P(None, 'tp')
- grad_w_out_t: float32 [512, 512], P('fsdp', 'tp')
- grad_b_out: float32 [512], replicated
- grad_ln2_gain: float32 [512], replicated
- grad_ln2_bias: float32 [512], replicated
- grad_w_up: float32 [512, 2048], P('fsdp', 'tp')
- grad_b_up: float32 [2048], P('tp')
- grad_w_down_t: float32 [512, 2048], P('fsdp', 'tp')
- grad_b_down: float32 [512], replicated
Inputs may be any that keep to these rules, and one draw needn't show every extreme that they name: `segment_ids`: in each sequence the ids never fall; each document has 1 to 512 characters and one has exactly 512.
All inputs are finite; a program needn't handle non-finite values.
Results may differ from a plain program's by a relative error of at most 0.011.
Values may be sent and summed in bfloat16 or wider, within the bound.
No kernel may reach another device: no remote copies, remote signals or barrier semaphores. Data moves between devices by JAX's collectives and lax.ppermute only.
A program may use at most 64 MiB of HBM per device.

v0:
```python
import jax
import jax.numpy as jnp
from jax import lax
from jax.sharding import PartitionSpec as P

HEAD_DIM = 64
EPSILON = 1e-05
NEGATIVE = -1e30
PRECISE = lax.Precision.HIGHEST


def layer_norm(values, norm_gain, norm_bias):
    centre = values - jnp.mean(values, axis=-1, keepdims=True)
    spread = jnp.mean(centre * centre, axis=-1, keepdims=True)
    return centre * lax.rsqrt(spread + EPSILON) * norm_gain + norm_bias


def contract_last(left, right):
    return lax.dot_general(
        left, right, (((1,), (1,)), ((), ())), preferred_element_type=jnp.float32
    )


def contract_first(left, right):
    return lax.dot_general(
        left, right, (((0,), (0,)), ((), ())), preferred_element_type=jnp.float32
    )


def per_device(
    layer_input,
    timesteps,
    segment_ids,
    time_table,
    ln1_gain,
    ln1_bias,
    w_qkv,
    b_qv,
    w_out_t,
    b_out,
    ln2_gain,
    ln2_bias,
    w_up,
    b_up,
    w_down_t,
    b_down,
    out_grad,
):
    seq_count, span_len, model_width = layer_input.shape
    tok_rows = seq_count * span_len
    seq_len = segment_ids.shape[1]
    step_count = time_table.shape[0]
    ctx_index = lax.axis_index("ctx")
    masters = (
        w_qkv.astype(jnp.bfloat16),
        w_out_t.astype(jnp.bfloat16),
        w_up.astype(jnp.bfloat16),
        w_down_t.astype(jnp.bfloat16),
    )
    qkv_mat, out_mat, up_mat, down_mat = (
        lax.all_gather(masters[0], "fsdp", axis=1, tiled=True),
        lax.all_gather(masters[1], "fsdp", axis=0, tiled=True),
        lax.all_gather(masters[2], "fsdp", axis=0, tiled=True),
        lax.all_gather(masters[3], "fsdp", axis=0, tiled=True),
    )
    steps_hot = (timesteps[:, None] == jnp.arange(step_count, dtype=jnp.int32)[None, :]).astype(
        jnp.float32
    )
    embedded = jnp.dot(steps_hot, time_table, precision=PRECISE)
    stream = (layer_input + embedded[:, None, :]).reshape(tok_rows, model_width)
    normed, norm_one_pull = jax.vjp(layer_norm, stream, ln1_gain, ln1_bias)
    normed_low = normed.astype(jnp.bfloat16)
    projected = jnp.einsum("rd,kdc->krc", normed_low, qkv_mat, preferred_element_type=jnp.float32)
    local_cols = projected.shape[2]
    heads_here = local_cols // HEAD_DIM
    query = (projected[0] + b_qv[0]).astype(jnp.bfloat16)
    key_local = projected[1].astype(jnp.bfloat16).reshape(seq_count, span_len, local_cols)
    value_local = (
        (projected[2] + b_qv[1]).astype(jnp.bfloat16).reshape(seq_count, span_len, local_cols)
    )
    key_all, value_all = (
        lax.all_gather(key_local, "ctx", axis=1, tiled=True),
        lax.all_gather(value_local, "ctx", axis=1, tiled=True),
    )
    query_ids = lax.dynamic_slice_in_dim(segment_ids, ctx_index * span_len, span_len, 1)
    same_doc = (query_ids[:, :, None] == segment_ids[:, None, :])[:, None]
    query_heads = query.reshape(seq_count, span_len, heads_here, HEAD_DIM)
    key_heads = key_all.reshape(seq_count, seq_len, heads_here, HEAD_DIM)
    value_heads = value_all.reshape(seq_count, seq_len, heads_here, HEAD_DIM)
    scale = HEAD_DIM ** (-0.5)

    def score_block():
        raw_scores = jnp.einsum(
            "sqhd,skhd->shqk", query_heads, key_heads, preferred_element_type=jnp.float32
        )
        return jnp.where(same_doc, raw_scores * scale, NEGATIVE)

    scores = score_block()
    row_top = jnp.max(scores, axis=-1, keepdims=True)
    expd = jnp.exp(scores - row_top)
    row_total = jnp.sum(expd, axis=-1, keepdims=True)
    probs = expd / row_total
    log_total = row_top + jnp.log(row_total)
    mixed = jnp.einsum(
        "shqk,skhd->sqhd",
        probs.astype(jnp.bfloat16),
        value_heads,
        preferred_element_type=jnp.float32,
    )
    mixed = mixed.reshape(tok_rows, local_cols).astype(jnp.bfloat16)
    attn_terms = contract_last(mixed, out_mat)
    attn = lax.psum(attn_terms, "tp")
    resid = stream + attn + b_out
    normed_two, norm_two_pull = jax.vjp(layer_norm, resid, ln2_gain, ln2_bias)
    normed_two_low = normed_two.astype(jnp.bfloat16)
    pre_act = jnp.dot(normed_two_low, up_mat, preferred_element_type=jnp.float32) + b_up
    activ, gelu_pull = jax.vjp(jax.nn.gelu, pre_act)
    activ_low = activ.astype(jnp.bfloat16)
    ffn_terms = contract_last(activ_low, down_mat)
    ffn = lax.psum(ffn_terms.astype(jnp.bfloat16), "tp").astype(jnp.float32)
    output = (resid + ffn + b_down).reshape(seq_count, span_len, model_width)
    cotan = out_grad.reshape(tok_rows, model_width)
    cotan_low = cotan.astype(jnp.bfloat16)
    grad_down = contract_first(cotan_low, activ_low)
    grad_act = jnp.dot(cotan_low, down_mat, preferred_element_type=jnp.float32)
    (grad_pre,) = gelu_pull(grad_act)
    grad_pre_low = grad_pre.astype(jnp.bfloat16)
    grad_upmat = contract_first(normed_two_low, grad_pre_low)
    back_two = lax.psum(contract_last(grad_pre_low, up_mat), "tp")
    resid_back, grad_gain_two, grad_bias_two = norm_two_pull(back_two)
    grad_resid = cotan + resid_back
    grad_resid_low = grad_resid.astype(jnp.bfloat16)
    grad_outmat = contract_first(grad_resid_low, mixed)
    grad_mixed = jnp.dot(grad_resid_low, out_mat, preferred_element_type=jnp.float32).astype(
        jnp.bfloat16
    )
    probs_again = jnp.exp(score_block() - log_total)
    mixed_heads = grad_mixed.reshape(seq_count, span_len, heads_here, HEAD_DIM)
    grad_probs = jnp.einsum(
        "sqhd,skhd->shqk", mixed_heads, value_heads, preferred_element_type=jnp.float32
    )
    inner = jnp.sum(probs_again * grad_probs, axis=-1, keepdims=True)
    grad_raw = (probs_again * (grad_probs - inner) * scale).astype(jnp.bfloat16)
    grad_query = jnp.einsum(
        "shqk,skhd->sqhd", grad_raw, key_heads, preferred_element_type=jnp.float32
    ).reshape(tok_rows, local_cols)
    grad_key_all = jnp.einsum(
        "shqk,sqhd->skhd", grad_raw, query_heads, preferred_element_type=jnp.float32
    ).reshape(seq_count, seq_len, local_cols)
    grad_value_all = jnp.einsum(
        "shqk,sqhd->skhd",
        probs_again.astype(jnp.bfloat16),
        mixed_heads,
        preferred_element_type=jnp.float32,
    ).reshape(seq_count, seq_len, local_cols)
    grad_key, grad_value = (
        lax.psum_scatter(grad_key_all, "ctx", scatter_dimension=1, tiled=True),
        lax.psum_scatter(grad_value_all, "ctx", scatter_dimension=1, tiled=True),
    )
    grad_key = grad_key.reshape(tok_rows, local_cols)
    grad_value = grad_value.reshape(tok_rows, local_cols)
    grad_stack = jnp.stack(
        [
            grad_query.astype(jnp.bfloat16),
            grad_key.astype(jnp.bfloat16),
            grad_value.astype(jnp.bfloat16),
        ]
    )
    grad_qkvmat = jnp.einsum(
        "rd,krc->kdc", normed_low, grad_stack, preferred_element_type=jnp.float32
    )
    back_one = lax.psum(
        jnp.einsum("krc,kdc->rd", grad_stack, qkv_mat, preferred_element_type=jnp.float32), "tp"
    )
    stream_back, grad_gain_one, grad_bias_one = norm_one_pull(back_one)
    grad_input = grad_resid + stream_back
    per_sequence = jnp.sum(grad_input.reshape(seq_count, span_len, model_width), axis=1)
    qv_terms = jnp.stack([jnp.sum(grad_query, axis=0), jnp.sum(grad_value, axis=0)])
    small = lax.psum(
        (
            grad_gain_one,
            grad_bias_one,
            grad_gain_two,
            grad_bias_two,
            qv_terms,
            jnp.sum(grad_pre, axis=0),
            jnp.sum(grad_resid, axis=0),
            jnp.sum(cotan, axis=0),
        ),
        ("fsdp", "ctx"),
    )
    (
        gain_one_sum,
        bias_one_sum,
        gain_two_sum,
        bias_two_sum,
        qv_sum,
        up_bias_sum,
        out_bias_sum,
        down_bias_sum,
    ) = small
    table_terms = jnp.dot(steps_hot.T, per_sequence, precision=PRECISE)
    table_sum = lax.psum(table_terms, ("fsdp", "ctx"))
    weight_terms = (grad_qkvmat, grad_outmat, grad_upmat, grad_down)
    summed = lax.psum((weight_terms[0], weight_terms[1], weight_terms[2], weight_terms[3]), "ctx")
    owned = (
        lax.psum_scatter(summed[0], "fsdp", scatter_dimension=1, tiled=True),
        lax.psum_scatter(summed[1], "fsdp", scatter_dimension=0, tiled=True),
        lax.psum_scatter(summed[2], "fsdp", scatter_dimension=0, tiled=True),
        lax.psum_scatter(summed[3], "fsdp", scatter_dimension=0, tiled=True),
    )
    qkv_owned, out_owned, up_owned, down_owned = owned
    return (
        output,
        grad_input.reshape(seq_count, span_len, model_width),
        table_sum,
        gain_one_sum,
        bias_one_sum,
        qkv_owned,
        qv_sum,
        out_owned,
        out_bias_sum,
        gain_two_sum,
        bias_two_sum,
        up_owned,
        up_bias_sum,
        down_owned,
        down_bias_sum,
    )


def solution(mesh):
    placed = (
        P("fsdp", "ctx", None),
        P("fsdp"),
        P("fsdp", None),
        P(),
        P(),
        P(),
        P(None, "fsdp", "tp"),
        P(None, "tp"),
        P("fsdp", "tp"),
        P(),
        P(),
        P(),
        P("fsdp", "tp"),
        P("tp"),
        P("fsdp", "tp"),
        P(),
        P("fsdp", "ctx", None),
    )
    return jax.shard_map(
        per_device,
        mesh=mesh,
        in_specs=placed,
        out_specs=(
            P("fsdp", "ctx", None),
            P("fsdp", "ctx", None),
            P(),
            P(),
            P(),
            P(None, "fsdp", "tp"),
            P(None, "tp"),
            P("fsdp", "tp"),
            P(),
            P(),
            P(),
            P("fsdp", "tp"),
            P("tp"),
            P("fsdp", "tp"),
            P(),
        ),
        check_vma=False,
    )
```

profile of v0, /device:TPU:0, one launch (start us, length us, event | category | flops | bytes accessed | tf_op | source)
XLA Modules:
  0.0 526.8 jit_solution(3402038133135190457)
XLA Ops:
  7.3 1.2 convert_element_type.111
  8.4 2.2 all_gather.18
  10.6 1.4 fusion.44
  12.1 1.4 fusion.62
  17.8 2.0 all_gather.21
  19.8 1.2 broadcast_compare_fusion
  21.0 2.1 reshape.228
  23.0 1.9 copy.60
  25.0 13.5 %all_gather.20 = bf16[2,1024,128]{2,1,0:T(8,128)(2,1)} all-gather(bf16[2,256,128]{2,1,0:T(8,128)(2,1)} %bitcast.102), channel_id=1, replica_groups=mesh['fsdp'=2,'ctx'=4,'tp'=4] {'ctx'}, dimensions={1}, use_global_device_ids=true | all-gather | bytes 655360 | tf_op jit(solution)/shard_map/all_gather | solution.py:82
  38.5 2.0 copy.61
  41.5 9.8 %all_gather.19 = bf16[2,1024,128]{2,1,0:T(8,128)(2,1)} all-gather(bf16[2,256,128]{2,1,0:T(8,128)(2,1)S(1)} %add_convert_fusion.3), channel_id=1, replica_groups=mesh['fsdp'=2,'ctx'=4,'tp'=4] {'ctx'}, dimensions={1}, use_global_device_ids=true | all-gather | bytes 655360 | tf_op jit(solution)/shard_map/all_gather | solution.py:83
  51.3 2.0 copy.58
  53.4 2.5 fusion.67
  55.9 1.1 fusion.2
  56.9 1.1 fusion.26
  58.8 1.3 fusion.70
  60.2 1.1 convert_element_type.121
  61.3 1.1 convert_element_type.123
  62.4 2.3 all_gather.22
  64.7 2.3 all_gather.23
  67.0 1.5 fusion.63
  69.4 1.4 fusion.71
  70.8 41.6 %all-reduce.9.cloned.1.call-done = f32[512,512]{1,0:T(8,128)} async-done(((f32[512,512]{1,0:T(8,128)}), f32[512,512]{1,0:T(8,128)}) %all-reduce.9.cloned.1.call-update) | async-done | bytes 1048592 | tf_op jit(solution)/shard_map/psum | solution.py:112
  112.4 1.5 fusion.60
  114.3 2.7 fusion.55
  117.8 1.4 fusion.41
  119.3 2.7 convolution_convert_fusion
  122.3 48.4 %all-reduce.13.cloned.1.call-done = f32[512,512]{1,0:T(8,128)} async-done(((f32[512,512]{1,0:T(8,128)}), f32[512,512]{1,0:T(8,128)}) %all-reduce.13.cloned.1.call-update) | async-done | bytes 1048592 | tf_op jit(solution)/shard_map/psum | solution.py:129
  170.6 2.0 multiply_reduce_fusion.1
  172.6 38.1 %all-reduce.11.cloned.1.call-done = bf16[512,512]{1,0:T(8,128)(2,1)} async-done(((bf16[512,512]{1,0:T(8,128)(2,1)}), bf16[512,512]{1,0:T(8,128)(2,1)}) %all-reduce.11.cloned.1.call-update) | async-done | bytes 524304 | tf_op jit(solution)/shard_map/psum | solution.py:120
  210.7 3.2 fusion.59
  214.1 1.1 copy-done.3
  216.1 1.7 reshape.230
  217.9 1.7 copy.64
  219.6 4.1 fusion.12
  223.7 3.8 fusion.72
  227.6 12.8 %fusion.7 = f32[2,2,64,1024]{3,2,1,0:T(8,128)} fusion(f32[2,2,256,1024]{3,2,1,0:T(8,128)} %fusion.72, f32[2,2,256,1024]{3,2,1,0:T(8,128)} %copy-done.1, f32[2,2,256]{2,1,0:T(2,128)S(1)} %log_add_fusion, f32[2,256,2,64]{1,3,2,0:T(8,128)} %copy.60, f32[2,64]{1,0:T(2,128)S(1)} %add.179), kind=kOutput, calls=%fused_computation.10 | convolution fusion | flops 141690880 | bytes 9703936 | tf_op jit(solution)/shard_map/shqk,sqhd->skhd/dot_general | solution.py:147
  240.5 2.3 fusion.36
  242.8 2.9 convolution_bitcast_fusion
  245.8 3.1 fusion.39
  248.9 12.1 %fusion.65 = (f32[2,64]{1,0:T(2,128)S(1)}, bf16[2,256,2,64]{1,3,2,0:T(8,128)(2,1)}) fusion(bf16[2,1024,2,64]{1,3,2,0:T(8,128)(2,1)} %bitcast.90, f32[2,2,256,1024]{3,2,1,0:T(8,128)} %fusion.72, f32[2,2,256,1024]{3,2,1,0:T(8,128)} %copy-done.1, f32[2,2,256]{2,1,0:T(2,128)S(1)} %log_add_fusion), kind=kOutput, calls=%fused_computation.104 | convolution fusion | flops 141690752 | bytes 9048576 | tf_op jit(solution)/shard_map/shqk,skhd->sqhd/dot_general | solution.py:144
  261.0 1.8 copy.76
  262.8 1.8 reshape.229
  264.6 1.7 fusion.66
  266.3 1.7 copy.68
  268.0 14.4 %reduce-scatter.7.cloned.1.call-done = f32[2,256,128]{1,2,0:T(8,128)} async-done(((f32[2,1024,128]{1,2,0:T(8,128)}), f32[2,256,128]{1,2,0:T(8,128)}) %reduce-scatter.7.cloned.1.call-update) | async-done | bytes 262160 | tf_op jit(solution)/shard_map/reduce_scatter | solution.py:157
  282.4 1.6 convert_element_type.133
  284.0 1.7 copy.66
  285.6 2.5 convolution_bitcast_fusion.2
  288.2 2.5 convolution_bitcast_fusion.1
  290.8 1.9 reduce-scatter.13.cloned.1.call-done
  292.7 12.1 %reduce-scatter.17.cloned.1.call-done = f32[256,512]{0,1:T(8,128)} async-done(((f32[512,512]{0,1:T(8,128)}), f32[256,512]{0,1:T(8,128)}) %reduce-scatter.17.cloned.1.call-update) | async-done | bytes 524304 | tf_op jit(solution)/shard_map/reduce_scatter | solution.py:210
  304.8 12.0 %reduce-scatter.15.cloned.1.call-done = f32[256,512]{1,0:T(8,128)} async-done(((f32[512,512]{1,0:T(8,128)}), f32[256,512]{1,0:T(8,128)}) %reduce-scatter.15.cloned.1.call-update) | async-done | bytes 524304 | tf_op jit(solution)/shard_map/reduce_scatter | solution.py:209
  316.7 12.3 %reduce-scatter.11.cloned.1.call-done = f32[3,256,128]{1,2,0:T(8,128)} async-done(((f32[3,512,128]{1,2,0:T(8,128)}), f32[3,256,128]{1,2,0:T(8,128)}) %reduce-scatter.11.cloned.1.call-update) | async-done | bytes 393232 | tf_op jit(solution)/shard_map/reduce_scatter | solution.py:207
  329.4 55.5 %all-reduce.15.cloned.1.call-done = f32[512,512]{1,0:T(8,128)} async-done(((f32[512,512]{1,0:T(8,128)}), f32[512,512]{1,0:T(8,128)}) %all-reduce.15.cloned.1.call-update) | async-done | bytes 1048592 | tf_op jit(solution)/shard_map/psum | solution.py:172
  384.9 1.8 multiply_reduce_fusion.2
  386.7 1.8 fusion.58
  388.7 2.4 fusion.43
  391.2 27.6 %all-reduce = (f32[512]{0:T(512)}, f32[512]{0:T(512)}, f32[2,128]{1,0:T(2,128)}, f32[512]{0:T(512)}, f32[512]{0:T(512)}, /*index=5*/f32[512]{0:T(512)}, f32[512]{0:T(512)}, f32[512]{0:T(512)}) all-reduce(f32[512]{0:T(512)S(1)} %get-tuple-element.62, ...), channel_id=1, replica_groups=mesh['fsdp'=2,'ctx'=4,'tp'=4] {'fsdp','ctx'}, use_global_device_ids=true, to_apply=%region_20.21 | all-reduce | flops 3840 | bytes 30720 | tf_op jit(solution)/shard_map/psum | solution.py:179
  418.9 31.2 %all-reduce.19.cloned.1.call-done = (f32[3,256,128]{1,2,0:T(8,128)}, f32[256,128]{1,0:T(8,128)}, f32[256,512]{1,0:T(8,128)}, f32[256,512]{0,1:T(8,128)}) async-done(((f32[3,256,128]{1,2,0:T(8,128)}, f32[256,128]{1,0:T(8,128)}, f32[256,512]{1,0:T(8,128)}, f32[256,512]{0,1:T(8,128)}), (f32[3,256,128]{1,2,0:T(8,128)}, f32[256,128]{1,0:T(8,128)}, f32[256,512]{1,0:T(8,128)}, ...) | async-done | bytes 1572880 | tf_op jit(solution)/shard_map/psum | solution.py:205
  450.1 1.9 copy.71
  452.1 2.0 copy.72
  454.1 61.3 %all-reduce.17.cloned.1.call-done = f32[1000,512]{1,0:T(8,128)} async-done(((f32[1000,512]{1,0:T(8,128)}), f32[1000,512]{1,0:T(8,128)}) %all-reduce.17.cloned.1.call-update) | async-done | bytes 2048016 | tf_op jit(solution)/shard_map/psum | solution.py:203
  515.4 3.1 copy.92
  (119 shorter events, 12.1 us)
Async XLA Ops:
  7.2 3.4 copy-start
  7.2 6.6 %copy-start.20 = (f32[512]{0:T(512)S(1)}, f32[512]{0:T(512)}, u32[]{:S(2)}) copy-start(f32[512]{0:T(512)} %param.21) | copy-start | bytes 6148
  7.2 6.6 %copy-start.22 = (f32[512]{0:T(512)S(1)}, f32[512]{0:T(512)}, u32[]{:S(2)}) copy-start(f32[512]{0:T(512)} %param.22) | copy-start | bytes 6148
  7.2 105.2 %all-reduce.9.cloned.1.call-start = ((), (), s32[]{:S(2)}) async-start(), calls=%async_computation.6 | async-start | bytes 2097152 | tf_op jit(solution)/shard_map/psum | solution.py:112
  12.0 4.7 copy-start.29
  12.0 7.8 %copy-start.21 = (s32[2,1024]{1,0:T(2,128)S(1)}, s32[2,1024]{1,0:T(2,128)}, u32[]{:S(2)}) copy-start(s32[2,1024]{1,0:T(2,128)} %param.19) | copy-start | bytes 24580
  14.0 0.8 copy-start.5
  53.4 3.6 copy-start.8
  55.8 2.2 copy-start.1
  56.9 1.9 copy-start.13
  58.2 0.7 copy-start.15
  60.1 52.3 %copy-start.23 = (f32[512]{0:T(512)S(1)}, f32[512]{0:T(512)}, u32[]{:S(2)}) copy-start(f32[512]{0:T(512)} %param.26) | copy-start | bytes 6148
  60.2 110.5 %all-reduce.13.cloned.1.call-start = ((), (), s32[]{:S(2)}) async-start(), calls=%async_computation.8 | async-start | bytes 2097152 | tf_op jit(solution)/shard_map/psum | solution.py:129
  64.7 49.5 %copy-start.19 = (f32[512]{0:T(512)S(1)}, f32[512]{0:T(512)}, u32[]{:S(2)}) copy-start(f32[512]{0:T(512)} %param.27) | copy-start | bytes 6148
  64.7 49.6 %copy-start.25 = (f32[512]{0:T(512)S(1)}, f32[512]{0:T(512)}, u32[]{:S(2)}) copy-start(f32[512]{0:T(512)} %param.28) | copy-start | bytes 6148
  64.7 49.6 %copy-start.30 = (f32[512]{0:T(512)S(1)}, f32[512]{0:T(512)}, u32[]{:S(2)}) copy-start(f32[512]{0:T(512)} %param.30) | copy-start | bytes 6148
  67.0 1.6 copy-start.11
  68.6 0.8 copy-start.10
  112.4 1.9 copy-start.12
  112.4 1.9 copy-start.16
  113.9 3.0 copy-start.2
  117.0 0.8 copy-start.9
  117.8 92.9 %copy-start.24 = (f32[512]{0:T(512)S(1)}, f32[512]{0:T(512)}, u32[]{:S(2)}) copy-start(f32[512]{0:T(512)} %param.32) | copy-start | bytes 6148
  119.3 91.4 %all-reduce.11.cloned.1.call-start = ((), (), s32[]{:S(2)}) async-start(), calls=%async_computation.7 | async-start | bytes 1048576 | tf_op jit(solution)/shard_map/psum | solution.py:120
  122.0 142.5 %reduce-scatter.9.cloned.1.call-start = ((), (), s32[]{:S(2)}) async-start(), calls=%async_computation.10 | async-start | bytes 1310720 | tf_op jit(solution)/shard_map/reduce_scatter | solution.py:158
  210.7 3.2 copy-start.6
  210.7 4.5 copy-start.14
  214.1 1.1 copy-start.3
  223.7 58.7 %reduce-scatter.7.cloned.1.call-start = ((), (), s32[]{:S(2)}) async-start(), calls=%async_computation.9 | async-start | bytes 1310720 | tf_op jit(solution)/shard_map/reduce_scatter | solution.py:157
  240.4 5.4 %copy-start.26 = (f32[512]{0:T(512)S(1)}, f32[512]{0:T(512)}, u32[]{:S(2)}) copy-start(f32[512]{0:T(512)} %param.28) | copy-start | bytes 6148
  240.4 52.3 %reduce-scatter.13.cloned.1.call-start = ((), (), s32[]{:S(2)}) async-start(), calls=%async_computation.14 | async-start | bytes 393216 | tf_op jit(solution)/shard_map/reduce_scatter | solution.py:208
  242.7 62.0 %reduce-scatter.17.cloned.1.call-start = ((), (), s32[]{:S(2)}) async-start(), calls=%async_computation.16 | async-start | bytes 1572864 | tf_op jit(solution)/shard_map/reduce_scatter | solution.py:210
  245.7 71.0 %reduce-scatter.15.cloned.1.call-start = ((), (), s32[]{:S(2)}) async-start(), calls=%async_computation.15 | async-start | bytes 1572864 | tf_op jit(solution)/shard_map/reduce_scatter | solution.py:209
  248.9 80.2 %reduce-scatter.11.cloned.1.call-start = ((), (), s32[]{:S(2)}) async-start(), calls=%async_computation.13 | async-start | bytes 1179648 | tf_op jit(solution)/shard_map/reduce_scatter | solution.py:207
  288.2 96.7 %all-reduce.15.cloned.1.call-start = ((), (), s32[]{:S(2)}) async-start(), calls=%async_computation.11 | async-start | bytes 2097152 | tf_op jit(solution)/shard_map/psum | solution.py:172
  290.7 159.4 %all-reduce.19.cloned.1.call-start = ((), (), s32[]{:S(2)}) async-start(), calls=%async_computation.17 | async-start | bytes 3145728 | tf_op jit(solution)/shard_map/psum | solution.py:205
  329.1 186.3 %all-reduce.17.cloned.1.call-start = ((), (), s32[]{:S(2)}) async-start(), calls=%async_computation.12 | async-start | bytes 4096000 | tf_op jit(solution)/shard_map/psum | solution.py:203
  384.9 3.6 copy-start.4
  386.6 2.1 copy-start.27
  388.4 2.8 copy-start.28
  388.6 129.9 %copy-start.7 = (f32[512,512]{1,0:T(8,128)}, f32[512,512]{1,0:T(8,128)S(1)}, u32[]{:S(2)}) copy-start(f32[512,512]{1,0:T(8,128)S(1)} %add_add_fusion.2) | copy-start | bytes 3145732
  450.1 68.4 %copy-start.18 = (f32[256,128]{1,0:T(8,128)S(1)}, f32[256,128]{1,0:T(8,128)}, u32[]{:S(2)}) copy-start(f32[256,128]{1,0:T(8,128)} %get-tuple-element.117) | copy-start | bytes 393220
  515.4 3.8 copy-start.17
Sparse Core Ops, SparseCore 0:
  60.3 52.0 all-reduce.8
  119.4 51.1 all-reduce.12
  173.0 37.6 all-reduce.10
  223.8 27.7 reduce-scatter.8
  254.6 27.7 reduce-scatter.6
  285.0 7.6 reduce-scatter.12
  295.0 9.6 reduce-scatter.16
  307.0 9.6 reduce-scatter.14
  319.7 9.3 reduce-scatter.10
  331.9 52.9 all-reduce.14
  388.6 61.4 all-reduce.18
  453.8 61.5 all-reduce.16
where the time goes:
time: 528 us; the launch traced here: 527 us
  waiting for transfers between devices  329 us (62%)
  matrix products  64.3 us (12%)
  blocking collectives  59.8 us (11%)
  local copies, waits for them, and re-layouts  33 us (6%)
  other arithmetic  25.2 us (5%)
  between operations  14.6 us (3%)
    psum x1, waiting for transfers between devices, per_device(): table_sum = lax.psum(table_terms, ('fsdp', 'ctx'))  61.3 us
    psum x1, waiting for transfers between devices, per_device(): lax.psum(jnp.einsum('krc,kdc->rd', grad_stack, qkv_mat, preferred_element...  55.5 us
    psum x1, waiting for transfers between devices, per_device(): back_two = lax.psum(contract_last(grad_pre_low, up_mat), 'tp')  48.4 us
    psum x1, waiting for transfers between devices, per_device(): attn = lax.psum(attn_terms, 'tp')  41.6 us
    psum x1, waiting for transfers between devices, per_device(): ffn = lax.psum(ffn_terms.astype(jnp.bfloat16), 'tp').astype(jnp.float32)  38.1 us
    psum x1, waiting for transfers between devices, per_device(): lax.psum((weight_terms[0], weight_terms[1], weight_terms[2], weight_terms...  31.2 us
    psum x1, blocking collectives, per_device(): lax.psum((grad_gain_one, grad_bias_one, grad_gain_two, grad_bias_two, qv_...  27.6 us
    reduce_scatter x1, waiting for transfers between devices, per_device(): lax.psum_scatter(grad_key_all, 'ctx', scatter_dimension=1, tiled=True)  14.4 us
  transfers between devices with their start and end apart: 12, of which 11 were waited for; matrix products, arithmetic and copies ran while one was open for 14% of the time, Pallas kernels for 0%

commit v1 on v0

--- a/solution.py
+++ b/solution.py
@@ -200,7 +200,7 @@
         down_bias_sum,
     ) = small
     table_terms = jnp.dot(steps_hot.T, per_sequence, precision=PRECISE)
-    table_sum = lax.psum(table_terms, ("fsdp", "ctx"))
+    table_sum = jnp.sum(lax.all_gather(table_terms, ("fsdp", "ctx")), axis=0)
     weight_terms = (grad_qkvmat, grad_outmat, grad_upmat, grad_down)
     summed = lax.psum((weight_terms[0], weight_terms[1], weight_terms[2], weight_terms[3]), "ctx")
     owned = (

time: 528 us -> 547 us (1.036)
  waiting for transfers between devices: 329 us -> 366 us
  local copies, waits for them, and re-layouts: 33 us -> 15.3 us
    all_gather x0 -> x1, waiting for transfers between devices: none -> 86.6 us  [per_device(): table_sum = jnp.sum(lax.all_gather(table_terms, ('fsdp', 'ctx')), axis=0)]
    psum x1 -> x0, waiting for transfers between devices: 61.3 us -> none  [per_device(): table_sum = lax.psum(table_terms, ('fsdp', 'ctx'))]
    reduce_sum x0 -> x1, other arithmetic: none -> 9.38 us  [per_device(): table_sum = jnp.sum(lax.all_gather(table_terms, ('fsdp', 'ctx')), axis=0)]
    reduce_scatter x1, waiting for transfers between devices: 14.4 us -> 20.7 us  [per_device(): lax.psum_scatter(grad_key_all, 'ctx', scatter_dimension=1, tiled=True)]
    unnamed x70 -> x65, local copies, waits for them, and re-layouts: 12.7 us -> 9.12 us
  transfers between devices with their start and end apart: 12 -> 12, of which waited for: 11 -> 11; matrix products, arithmetic and copies ran while one was open for 14% -> 11% of each run, Pallas kernels for 0% -> 0%
where the time goes in v1:
time: 547 us; the launch traced here: 545 us
  waiting for transfers between devices  366 us (67%)
  matrix products  59.7 us (11%)
  blocking collectives  58.4 us (11%)
  other arithmetic  30.6 us (6%)
  local copies, waits for them, and re-layouts  15.3 us (3%)
  between operations  14.7 us (3%)
    all_gather x1, waiting for transfers between devices, per_device(): table_sum = jnp.sum(lax.all_gather(table_terms, ('fsdp', 'ctx')), axis=0)  86.6 us
    psum x1, waiting for transfers between devices, per_device(): lax.psum(jnp.einsum('krc,kdc->rd', grad_stack, qkv_mat, preferred_element...  55.5 us
    psum x1, waiting for transfers between devices, per_device(): back_two = lax.psum(contract_last(grad_pre_low, up_mat), 'tp')  48.4 us
    psum x1, waiting for transfers between devices, per_device(): attn = lax.psum(attn_terms, 'tp')  43 us
    psum x1, waiting for transfers between devices, per_device(): ffn = lax.psum(ffn_terms.astype(jnp.bfloat16), 'tp').astype(jnp.float32)  39 us
    psum x1, waiting for transfers between devices, per_device(): lax.psum((weight_terms[0], weight_terms[1], weight_terms[2], weight_terms...  30.3 us
    psum x1, blocking collectives, per_device(): lax.psum((grad_gain_one, grad_bias_one, grad_gain_two, grad_bias_two, qv_...  27.7 us
    reduce_scatter x1, waiting for transfers between devices, per_device(): lax.psum_scatter(grad_key_all, 'ctx', scatter_dimension=1, tiled=True)  20.7 us
  transfers between devices with their start and end apart: 12, of which 11 were waited for; matrix products, arithmetic and copies ran while one was open for 11% of the time, Pallas kernels for 0%

profile of v1, /device:TPU:0, one launch (start us, length us, event | category | flops | bytes accessed | tf_op | source)
XLA Modules:
  0.0 545.5 jit_solution(15708354884964933504)
XLA Ops:
  7.3 1.2 convert_element_type.111
  8.4 2.2 all_gather.24
  10.6 1.4 fusion.44
  12.1 1.4 fusion.62
  14.5 0.7 slice.27
  15.2 0.7 fusion.64
  16.0 1.9 all_gather.27
  18.0 1.2 broadcast_compare_fusion
  19.6 12.3 %all_gather.26 = bf16[2,1024,128]{2,1,0:T(8,128)(2,1)S(1)} all-gather(bf16[2,256,128]{2,1,0:T(8,128)(2,1)} %bitcast.104), channel_id=1, replica_groups=mesh['fsdp'=2,'ctx'=4,'tp'=4] {'ctx'}, dimensions={1}, use_global_device_ids=true | all-gather | bytes 655360 | tf_op jit(solution)/shard_map/all_gather | solution.py:82
  32.1 1.2 add_convert_fusion.3
  33.3 9.8 %all_gather.25 = bf16[2,1024,128]{2,1,0:T(8,128)(2,1)} all-gather(bf16[2,256,128]{2,1,0:T(8,128)(2,1)S(1)} %add_convert_fusion.3), channel_id=1, replica_groups=mesh['fsdp'=2,'ctx'=4,'tp'=4] {'ctx'}, dimensions={1}, use_global_device_ids=true | all-gather | bytes 655360 | tf_op jit(solution)/shard_map/all_gather | solution.py:83
  43.1 1.2 copy.58
  44.4 2.4 fusion.67
  46.8 1.1 fusion.2
  47.8 1.1 fusion.26
  49.1 1.3 fusion.70
  50.5 1.1 convert_element_type.121
  51.6 1.1 convert_element_type.123
  52.6 2.3 all_gather.28
  55.0 2.3 all_gather.29
  57.4 0.7 copy-done.12
  58.2 1.4 fusion.71
  59.6 43.0 %all-reduce.8.cloned.1.call-done = f32[512,512]{1,0:T(8,128)} async-done(((f32[512,512]{1,0:T(8,128)}), f32[512,512]{1,0:T(8,128)}) %all-reduce.8.cloned.1.call-update) | async-done | bytes 1048592 | tf_op jit(solution)/shard_map/psum | solution.py:112
  102.7 1.5 fusion.60
  104.5 2.1 fusion.55
  106.7 0.8 copy-done.10
  107.5 1.4 fusion.41
  109.0 2.7 convolution_convert_fusion
  112.0 48.4 %all-reduce.12.cloned.1.call-done = f32[512,512]{1,0:T(8,128)} async-done(((f32[512,512]{1,0:T(8,128)}), f32[512,512]{1,0:T(8,128)}) %all-reduce.12.cloned.1.call-update) | async-done | bytes 1048592 | tf_op jit(solution)/shard_map/psum | solution.py:129
  160.3 1.6 multiply_reduce_fusion.1
  162.0 39.0 %all-reduce.10.cloned.1.call-done = bf16[512,512]{1,0:T(8,128)(2,1)} async-done(((bf16[512,512]{1,0:T(8,128)(2,1)}), bf16[512,512]{1,0:T(8,128)(2,1)}) %all-reduce.10.cloned.1.call-update) | async-done | bytes 524304 | tf_op jit(solution)/shard_map/psum | solution.py:120
  201.0 2.9 fusion.59
  204.1 1.0 copy-done.3
  205.3 0.8 reshape.231
  206.2 1.1 copy.64
  207.2 4.1 fusion.12
  211.4 3.8 fusion.72
  215.2 12.8 %fusion.7 = f32[2,2,64,1024]{3,2,1,0:T(8,128)} fusion(f32[2,2,256,1024]{3,2,1,0:T(8,128)} %fusion.72, f32[2,2,256,1024]{3,2,1,0:T(8,128)} %copy-done.2, f32[2,2,256]{2,1,0:T(2,128)S(1)} %log_add_fusion, f32[2,256,2,64]{1,3,2,0:T(8,128)} %copy-done.14, f32[2,64]{1,0:T(2,128)S(1)} %add.177), kind=kOutput, calls=%fused_computation.10 | convolution fusion | flops 141690880 | bytes 9703936 | tf_op jit(solution)/shard_map/shqk,sqhd->skhd/dot_general | solution.py:147
  228.1 2.3 fusion.36
  230.4 2.9 convolution_bitcast_fusion
  233.4 2.7 fusion.39
  236.1 11.5 %fusion.65 = (f32[2,64]{1,0:T(2,128)S(1)}, bf16[2,256,2,64]{1,3,2,0:T(8,128)(2,1)S(1)}) fusion(bf16[2,1024,2,64]{1,3,2,0:T(8,128)(2,1)} %bitcast.92, f32[2,2,256,1024]{3,2,1,0:T(8,128)} %fusion.72, f32[2,2,256,1024]{3,2,1,0:T(8,128)} %copy-done.2, f32[2,2,256]{2,1,0:T(2,128)S(1)} %log_add_fusion), kind=kOutput, calls=%fused_computation.104 | convolution fusion | flops 141690752 | bytes 9048576 | tf_op jit(solution)/shard_map/shqk,skhd->sqhd/dot_general | solution.py:144
  248.0 1.2 fusion.66
  249.4 20.7 %reduce-scatter.7.cloned.1.call-done = f32[2,256,128]{1,2,0:T(8,128)} async-done(((f32[2,1024,128]{1,2,0:T(8,128)}), f32[2,256,128]{1,2,0:T(8,128)}) %reduce-scatter.7.cloned.1.call-update) | async-done | bytes 262160 | tf_op jit(solution)/shard_map/reduce_scatter | solution.py:157
  270.1 1.0 convert_element_type.133
  271.2 1.3 convolution_bitcast_fusion.2
  272.5 1.4 convolution_bitcast_fusion.1
  274.0 6.4 %reduce-scatter.13.cloned.1.call-done = f32[256,128]{1,0:T(8,128)} async-done(((f32[512,128]{1,0:T(8,128)}), f32[256,128]{1,0:T(8,128)}) %reduce-scatter.13.cloned.1.call-update) | async-done | bytes 131088 | tf_op jit(solution)/shard_map/reduce_scatter | solution.py:208
  280.4 12.1 %reduce-scatter.17.cloned.1.call-done = f32[256,512]{0,1:T(8,128)} async-done(((f32[512,512]{0,1:T(8,128)}), f32[256,512]{0,1:T(8,128)}) %reduce-scatter.17.cloned.1.call-update) | async-done | bytes 524304 | tf_op jit(solution)/shard_map/reduce_scatter | solution.py:210
  292.5 12.0 %reduce-scatter.15.cloned.1.call-done = f32[256,512]{1,0:T(8,128)} async-done(((f32[512,512]{1,0:T(8,128)}), f32[256,512]{1,0:T(8,128)}) %reduce-scatter.15.cloned.1.call-update) | async-done | bytes 524304 | tf_op jit(solution)/shard_map/reduce_scatter | solution.py:209
  304.4 11.8 %reduce-scatter.11.cloned.1.call-done = f32[3,256,128]{1,2,0:T(8,128)} async-done(((f32[3,512,128]{1,2,0:T(8,128)}), f32[3,256,128]{1,2,0:T(8,128)}) %reduce-scatter.11.cloned.1.call-update) | async-done | bytes 393232 | tf_op jit(solution)/shard_map/reduce_scatter | solution.py:207
  316.5 55.5 %all-reduce.14.cloned.1.call-done = f32[512,512]{1,0:T(8,128)} async-done(((f32[512,512]{1,0:T(8,128)}), f32[512,512]{1,0:T(8,128)}) %all-reduce.14.cloned.1.call-update) | async-done | bytes 1048592 | tf_op jit(solution)/shard_map/psum | solution.py:172
  372.0 1.7 multiply_reduce_fusion.2
  373.7 1.8 fusion.58
  375.7 1.0 copy-done.7
  376.8 2.4 fusion.43
  379.3 27.7 %all-reduce = (f32[512]{0:T(512)}, f32[512]{0:T(512)}, f32[2,128]{1,0:T(2,128)}, f32[512]{0:T(512)}, f32[512]{0:T(512)}, /*index=5*/f32[512]{0:T(512)}, f32[512]{0:T(512)}, f32[512]{0:T(512)}) all-reduce(f32[512]{0:T(512)S(1)} %get-tuple-element.62, ...), channel_id=1, replica_groups=mesh['fsdp'=2,'ctx'=4,'tp'=4] {'fsdp','ctx'}, use_global_device_ids=true, to_apply=%region_20.21 | all-reduce | flops 3840 | bytes 30720 | tf_op jit(solution)/shard_map/psum | solution.py:179
  406.9 30.3 %all-reduce.16.cloned.1.call-done = (f32[3,256,128]{1,2,0:T(8,128)}, f32[256,128]{1,0:T(8,128)}, f32[256,512]{1,0:T(8,128)}, f32[256,512]{0,1:T(8,128)}) async-done(((f32[3,256,128]{1,2,0:T(8,128)}, f32[256,128]{1,0:T(8,128)}, f32[256,512]{1,0:T(8,128)}, f32[256,512]{0,1:T(8,128)}), (f32[3,256,128]{1,2,0:T(8,128)}, f32[256,128]{1,0:T(8,128)}, f32[256,512]{1,0:T(8,128)}, ...) | async-done | bytes 1572880 | tf_op jit(solution)/shard_map/psum | solution.py:205
  437.2 1.9 copy.71
  439.2 2.0 copy.72
  441.2 86.6 %all-gather.3.cloned.1.call-done = f32[8000,512]{1,0:T(8,128)} async-done(((f32[1000,512]{1,0:T(8,128)}), f32[8000,512]{1,0:T(8,128)}) %all-gather.3.cloned.1.call-update) | async-done | bytes 16384016 | tf_op jit(solution)/shard_map/all_gather | solution.py:203
  527.8 9.4 %reduce_sum.232 = f32[1000,512]{1,0:T(8,128)} reduce(f32[8,1000,512]{2,1,0:T(8,128)} %bitcast.88, f32[]{:T(128)} %constant.11.clone.1), dimensions={0}, to_apply=%region_18.19 | reduce | flops 3584000 | bytes 18432004 | tf_op jit(solution)/shard_map/reduce_sum | solution.py:203
  537.2 0.7 copy.91
  537.8 0.8 copy.92
  (115 shorter events, 5.2 us)
Async XLA Ops:
  7.2 3.4 copy-start
  7.2 6.6 %copy-start.20 = (f32[512]{0:T(512)S(1)}, f32[512]{0:T(512)}, u32[]{:S(2)}) copy-start(f32[512]{0:T(512)} %param.21) | copy-start | bytes 6148
  7.2 6.6 %copy-start.22 = (f32[512]{0:T(512)S(1)}, f32[512]{0:T(512)}, u32[]{:S(2)}) copy-start(f32[512]{0:T(512)} %param.22) | copy-start | bytes 6148
  7.2 95.5 %all-reduce.8.cloned.1.call-start = ((), (), s32[]{:S(2)}) async-start(), calls=%async_computation.6 | async-start | bytes 2097152 | tf_op jit(solution)/shard_map/psum | solution.py:112
  12.0 3.9 copy-start.27
  12.1 4.0 copy-start.17
  12.1 5.9 %copy-start.21 = (s32[2,1024]{1,0:T(2,128)S(1)}, s32[2,1024]{1,0:T(2,128)}, u32[]{:S(2)}) copy-start(s32[2,1024]{1,0:T(2,128)} %param.19) | copy-start | bytes 24580
  19.6 27.1 %copy-start.14 = (f32[2,256,2,64]{1,3,2,0:T(8,128)}, f32[2,256,2,64]{1,3,2,0:T(8,128)S(1)}, u32[]{:S(2)}) copy-start(f32[2,256,2,64]{1,3,2,0:T(8,128)S(1)} %copy.60) | copy-start | bytes 786436
  32.1 15.7 %copy-start.8 = (bf16[2,1024,128]{1,2,0:T(8,128)(2,1)}, bf16[2,1024,128]{1,2,0:T(8,128)(2,1)S(1)}, u32[]{:S(2)}) copy-start(bf16[2,1024,128]{1,2,0:T(8,128)(2,1)S(1)} %copy.61) | copy-start | bytes 1572868
  44.4 3.5 copy-start.9
  46.8 2.2 copy-start.2
  48.9 8.3 %copy-start.5 = (f32[2,256,512]{2,1,0:T(8,128)S(1)}, f32[2,256,512]{2,1,0:T(8,128)}, u32[]{:S(2)}) copy-start(f32[2,256,512]{2,1,0:T(8,128)} %param.33) | copy-start | bytes 3145732
  50.4 52.3 %copy-start.23 = (f32[512]{0:T(512)S(1)}, f32[512]{0:T(512)}, u32[]{:S(2)}) copy-start(f32[512]{0:T(512)} %param.26) | copy-start | bytes 6148
  50.4 109.9 %all-reduce.12.cloned.1.call-start = ((), (), s32[]{:S(2)}) async-start(), calls=%async_computation.8 | async-start | bytes 2097152 | tf_op jit(solution)/shard_map/psum | solution.py:129
  54.9 49.5 %copy-start.19 = (f32[512]{0:T(512)S(1)}, f32[512]{0:T(512)}, u32[]{:S(2)}) copy-start(f32[512]{0:T(512)} %param.27) | copy-start | bytes 6148
  55.0 49.5 %copy-start.25 = (f32[512]{0:T(512)S(1)}, f32[512]{0:T(512)}, u32[]{:S(2)}) copy-start(f32[512]{0:T(512)} %param.28) | copy-start | bytes 6148
  55.0 49.6 %copy-start.28 = (f32[512]{0:T(512)S(1)}, f32[512]{0:T(512)}, u32[]{:S(2)}) copy-start(f32[512]{0:T(512)} %param.30) | copy-start | bytes 6148
  57.3 0.8 copy-start.12
  57.4 0.8 copy-start.11
  102.7 1.8 copy-start.13
  102.7 1.8 copy-start.15
  106.7 0.8 copy-start.10
  107.5 93.5 %copy-start.24 = (f32[512]{0:T(512)S(1)}, f32[512]{0:T(512)}, u32[]{:S(2)}) copy-start(f32[512]{0:T(512)} %param.32) | copy-start | bytes 6148
  109.0 92.0 %all-reduce.10.cloned.1.call-start = ((), (), s32[]{:S(2)}) async-start(), calls=%async_computation.7 | async-start | bytes 1048576 | tf_op jit(solution)/shard_map/psum | solution.py:120
  111.7 136.3 %reduce-scatter.9.cloned.1.call-start = ((), (), s32[]{:S(2)}) async-start(), calls=%async_computation.10 | async-start | bytes 1310720 | tf_op jit(solution)/shard_map/reduce_scatter | solution.py:158
  201.0 2.9 copy-start.6
  204.1 1.0 copy-start.3
  211.4 58.7 %reduce-scatter.7.cloned.1.call-start = ((), (), s32[]{:S(2)}) async-start(), calls=%async_computation.9 | async-start | bytes 1310720 | tf_op jit(solution)/shard_map/reduce_scatter | solution.py:157
  228.0 52.4 %reduce-scatter.13.cloned.1.call-start = ((), (), s32[]{:S(2)}) async-start(), calls=%async_computation.14 | async-start | bytes 393216 | tf_op jit(solution)/shard_map/reduce_scatter | solution.py:208
  230.4 62.1 %reduce-scatter.17.cloned.1.call-start = ((), (), s32[]{:S(2)}) async-start(), calls=%async_computation.16 | async-start | bytes 1572864 | tf_op jit(solution)/shard_map/reduce_scatter | solution.py:210
  233.3 71.1 %reduce-scatter.15.cloned.1.call-start = ((), (), s32[]{:S(2)}) async-start(), calls=%async_computation.15 | async-start | bytes 1572864 | tf_op jit(solution)/shard_map/reduce_scatter | solution.py:209
  236.1 80.1 %reduce-scatter.11.cloned.1.call-start = ((), (), s32[]{:S(2)}) async-start(), calls=%async_computation.13 | async-start | bytes 1179648 | tf_op jit(solution)/shard_map/reduce_scatter | solution.py:207
  272.5 99.5 %all-reduce.14.cloned.1.call-start = ((), (), s32[]{:S(2)}) async-start(), calls=%async_computation.11 | async-start | bytes 2097152 | tf_op jit(solution)/shard_map/psum | solution.py:172
  274.0 101.5 %copy-start.4 = (f32[512,512]{1,0:T(8,128)S(1)}, f32[512,512]{1,0:T(8,128)}, u32[]{:S(2)}) copy-start(f32[512,512]{1,0:T(8,128)} %copy-done.3) | copy-start | bytes 3145732
  274.0 163.3 %all-reduce.16.cloned.1.call-start = ((), (), s32[]{:S(2)}) async-start(), calls=%async_computation.17 | async-start | bytes 3145728 | tf_op jit(solution)/shard_map/psum | solution.py:205
  316.3 211.5 %all-gather.3.cloned.1.call-start = ((), (), s32[]{:S(2)}) async-start(), calls=%async_computation.12 | async-start | bytes 18432000 | tf_op jit(solution)/shard_map/all_gather | solution.py:203
  373.7 3.1 copy-start.26
  375.7 1.0 copy-start.7
  527.8 9.4 %copy-start.18 = (f32[256,128]{1,0:T(8,128)S(1)}, f32[256,128]{1,0:T(8,128)}, u32[]{:S(2)}) copy-start(f32[256,128]{1,0:T(8,128)} %get-tuple-element.117) | copy-start | bytes 393220
  527.8 10.0 %copy-start.16 = (f32[256,512]{1,0:T(8,128)S(1)}, f32[256,512]{1,0:T(8,128)}, u32[]{:S(2)}) copy-start(f32[256,512]{1,0:T(8,128)} %get-tuple-element.121) | copy-start | bytes 1572868
  527.8 10.8 %copy-start.1 = (f32[1000,512]{1,0:T(8,128)S(1)}, f32[1000,512]{1,0:T(8,128)}, u32[]{:S(2)}) copy-start(f32[1000,512]{1,0:T(8,128)} %param.20) | copy-start | bytes 6144004
Sparse Core Ops, SparseCore 0:
  50.5 52.0 all-reduce.7
  109.1 51.1 all-reduce.11
  163.3 37.6 all-reduce.9
  211.5 27.7 reduce-scatter.8
  242.2 27.7 reduce-scatter.6
  272.7 7.6 reduce-scatter.12
  282.8 9.6 reduce-scatter.16
  294.7 9.6 reduce-scatter.14
  306.8 9.3 reduce-scatter.10
  319.0 52.9 all-reduce.13
  375.7 61.4 all-reduce.15
  439.6 88.1 all-gather.2
